TPU v7x, 32 devices: a whole 2x2x4 slice. The times are simulated.
32 devices in a mesh: dp: 2 (over y), tensor: 16 (over z, x, core).
Axes of the slice: x: 2, y: 2, z: 4, core: 2. Of those that a mesh axis runs over, the one named last changes fastest.
Arguments:
- inputs: float32 [256, 4096], P('dp', 'tensor'), may hold values from -6 to 6
- out_grad: float32 [256, 4096], P('dp', 'tensor'), may hold values from -6 to 6
- up_weight: float32 [768, 128, 128], P('tensor'), may hold values from -0.25 to 0.25
- down_weight: float32 [768, 128, 128], P('tensor'), may hold values from -0.109375 to 0.109375
- up_left: float32 [4096, 128], P('tensor'), may hold values from -0.09375 to 0.09375
- up_right: float32 [128, 16384], P(None, 'tensor'), may hold values from -0.5 to 0.5
- down_left: float32 [16384, 128], P('tensor'), may hold values from -0.046875 to 0.046875
- down_right: float32 [128, 4096], P(None, 'tensor'), may hold values from -0.5 to 0.5
- model_block: int32 [768], P('tensor'), may hold values from 0 to 31, as said below
- hidden_block: int32 [768], P('tensor'), may hold values from 0 to 7
- live_slots: int32 [16], P('tensor'), may hold values from 24 to 48, as said below
Outputs:
- result: float32 [256, 4096], P('dp', 'tensor')
- input_grad: float32 [256, 4096], P('dp', 'tensor')
- up_grad: float32 [768, 128, 128], P('tensor', 'dp')
- down_grad: float32 [768, 128, 128], P('tensor', 'dp')
- up_left_grad: float32 [4096, 128], P(('tensor', 'dp'))
- up_right_grad: float32 [128, 16384], P('dp', 'tensor')
- down_left_grad: float32 [16384, 128], P(('tensor', 'dp'))
- down_right_grad: float32 [128, 4096], P('dp', 'tensor')
Inputs may be any that keep to these rules, and one draw needn't show every extreme that they name: `model_block`: with g the slot's hidden block counted over all owners, the slot's model block differs from g mod 32 in at most one bit. `live_slots`: at least one owner has all 48 slots live.
All inputs are finite; a program needn't handle non-finite values.
Results may differ from a plain program's by a relative error of at most 0.0003.
Values sent between devices are 32-bit elements; how exact they have to be, the bound alone decides.
A program may use at most 64 MiB of HBM per device.

v0:
```python
import jax
import jax.numpy as jnp
from jax import lax
from jax.sharding import PartitionSpec as P

highest = lax.Precision.HIGHEST


def activation(values):
    return jax.nn.gelu(values, approximate=True)


def onehot(indices, extent):
    return (indices[:, None] == jnp.arange(extent, dtype=jnp.int32)[None, :]).astype(jnp.float32)


def spread_cols(field):
    return lax.all_gather(field, "tensor", axis=1, tiled=True)


def rank_total(partial_value):
    return lax.psum(partial_value, "tensor")


def block_total(partial_value):
    return lax.psum_scatter(partial_value, "tensor", scatter_dimension=1, tiled=True)


def shards(
    inputs,
    out_grad,
    up_weight,
    down_weight,
    up_left,
    up_right,
    down_left,
    down_right,
    model_block,
    hidden_block,
    live_slots,
):
    row_count = inputs.shape[0]
    slot_count = up_weight.shape[0]
    block_size = up_weight.shape[1]
    hidden_width = up_right.shape[1]
    local_blocks = hidden_width // block_size
    model_width = inputs.shape[1] * lax.axis_size("tensor")
    model_blocks = model_width // block_size
    alive_mask = (jnp.arange(slot_count, dtype=jnp.int32) < live_slots[0]).astype(jnp.float32)
    up_live = up_weight * alive_mask[:, None, None]
    down_live = down_weight * alive_mask[:, None, None]
    hidden_hot = onehot(hidden_block, local_blocks)
    model_hot = onehot(model_block, model_blocks)
    inputs_full = spread_cols(inputs)
    split_in = inputs_full.reshape(row_count, model_blocks, block_size)
    chosen_in = jnp.take(split_in, model_block, axis=1)
    slot_out = jnp.einsum("tsk,skn->tsn", chosen_in, up_live, precision=highest)
    low_in = rank_total(jnp.dot(inputs, up_left, precision=highest))
    merged = jnp.einsum("tsn,sh->thn", slot_out, hidden_hot, precision=highest)
    preact = merged.reshape(row_count, hidden_width) + jnp.dot(low_in, up_right, precision=highest)
    hidden = activation(preact)
    chosen_hidden = jnp.take(
        hidden.reshape(row_count, local_blocks, block_size), hidden_block, axis=1
    )
    slot_down = jnp.einsum("tsk,skn->tsn", chosen_hidden, down_live, precision=highest)
    placed = jnp.einsum("tsn,sm->tmn", slot_down, model_hot, precision=highest)
    low_mid = rank_total(jnp.dot(hidden, down_left, precision=highest))
    result = block_total(placed.reshape(row_count, model_width)) + jnp.dot(
        low_mid, down_right, precision=highest
    )
    grad_full = spread_cols(out_grad)
    back_mid = rank_total(jnp.dot(out_grad, down_right.T, precision=highest))
    chosen_grad = jnp.take(
        grad_full.reshape(row_count, model_blocks, block_size), model_block, axis=1
    )
    slot_back = jnp.einsum("tsn,skn->tsk", chosen_grad, down_live, precision=highest)
    merged_back = jnp.einsum("tsk,sh->thk", slot_back, hidden_hot, precision=highest)
    hidden_grad = merged_back.reshape(row_count, hidden_width) + jnp.dot(
        back_mid, down_left.T, precision=highest
    )
    _, pullback = jax.vjp(activation, preact)
    preact_grad = pullback(hidden_grad)[0]
    down_grad = (
        jnp.einsum("tsk,tsn->skn", chosen_hidden, chosen_grad, precision=highest)
        * alive_mask[:, None, None]
    )
    down_left_grad = jnp.dot(hidden.T, back_mid, precision=highest)
    down_right_grad = jnp.dot(low_mid.T, out_grad, precision=highest)
    chosen_pgrad = jnp.take(
        preact_grad.reshape(row_count, local_blocks, block_size), hidden_block, axis=1
    )
    slot_in = jnp.einsum("tsn,skn->tsk", chosen_pgrad, up_live, precision=highest)
    placed_in = jnp.einsum("tsk,sm->tmk", slot_in, model_hot, precision=highest)
    back_in = rank_total(jnp.dot(preact_grad, up_right.T, precision=highest))
    input_grad = block_total(placed_in.reshape(row_count, model_width)) + jnp.dot(
        back_in, up_left.T, precision=highest
    )
    up_grad = (
        jnp.einsum("tsk,tsn->skn", chosen_in, chosen_pgrad, precision=highest)
        * alive_mask[:, None, None]
    )
    up_left_grad = jnp.dot(inputs.T, back_in, precision=highest)
    up_right_grad = jnp.dot(low_in.T, preact_grad, precision=highest)
    up_grad, down_grad, up_left_grad, up_right_grad, down_left_grad, down_right_grad = (
        lax.psum_scatter(up_grad, "dp", scatter_dimension=1, tiled=True),
        lax.psum_scatter(down_grad, "dp", scatter_dimension=1, tiled=True),
        lax.psum_scatter(up_left_grad, "dp", scatter_dimension=0, tiled=True),
        lax.psum_scatter(up_right_grad, "dp", scatter_dimension=0, tiled=True),
        lax.psum_scatter(down_left_grad, "dp", scatter_dimension=0, tiled=True),
        lax.psum_scatter(down_right_grad, "dp", scatter_dimension=0, tiled=True),
    )
    return (
        result,
        input_grad,
        up_grad,
        down_grad,
        up_left_grad,
        up_right_grad,
        down_left_grad,
        down_right_grad,
    )


def solution(mesh):
    return jax.shard_map(
        shards,
        mesh=mesh,
        in_specs=(
            P("dp", "tensor"),
            P("dp", "tensor"),
            P("tensor", None, None),
            P("tensor", None, None),
            P("tensor", None),
            P(None, "tensor"),
            P("tensor", None),
            P(None, "tensor"),
            P("tensor"),
            P("tensor"),
            P("tensor"),
        ),
        out_specs=(
            P("dp", "tensor"),
            P("dp", "tensor"),
            P("tensor", "dp", None),
            P("tensor", "dp", None),
            P(("tensor", "dp"), None),
            P("dp", "tensor"),
            P(("tensor", "dp"), None),
            P("dp", "tensor"),
        ),
        check_vma=False,
    )
```

profile of v0, /device:TPU:0, one launch (start us, length us, event | category | flops | bytes accessed | tf_op | source)
XLA Modules:
  0.0 594.8 jit_solution(16330252394450351353)
XLA Ops:
  7.2 1.7 copy.25
  9.0 1.7 copy.32
  10.7 1.9 fusion.103
  12.6 1.9 fusion.104
  17.9 37.0 %all-gather.3.cloned.1.call-done = f32[128,4096]{0,1:T(8,128)} async-done(((f32[128,256]{0,1:T(8,128)}), f32[128,4096]{0,1:T(8,128)}) %all-gather.3.cloned.1.call-update) | async-done | bytes 2097168 | tf_op jit(solution)/shard_map/all_gather | solution.py:18
  54.9 1.9 copy.26
  56.9 2.4 gather_fusion
  59.2 10.4 %fusion.26 = f32[128,48,128]{0,2,1:T(8,128)} fusion(f32[48,128,128]{2,1,0:T(8,128)} %gather_fusion, f32[48,128,128]{2,1,0:T(8,128)} %param.17, f32[48]{0:T(128)S(1)} %get-tuple-element.39, pred[48]{0:T(512)(128)(4,1)S(1)} %get-tuple-element.38), kind=kOutput, calls=%fused_computation.32 | convolution fusion | flops 1209532416 | bytes 9437424 | tf_op jit(solution)/shard_map/tsk,skn->tsn/dot_general | solution.py:57
  69.7 3.6 copy.28
  73.3 3.8 fusion.90
  77.1 20.8 %all-gather.5.cloned.1.call-done = f32[128,4096]{0,1:T(8,128)} async-done(((f32[128,256]{0,1:T(8,128)}), f32[128,4096]{0,1:T(8,128)}) %all-gather.5.cloned.1.call-update) | async-done | bytes 2097168 | tf_op jit(solution)/shard_map/all_gather | solution.py:18
  97.9 1.9 copy.33
  99.8 2.4 gather_fusion.2
  102.2 86.9 %all-reduce.7.cloned.1.call-done = (f32[128,128]{1,0:T(8,128)}, f32[128,128]{1,0:T(8,128)}) async-done(((f32[128,128]{1,0:T(8,128)}, f32[128,128]{1,0:T(8,128)}), (f32[128,128]{1,0:T(8,128)}, f32[128,128]{1,0:T(8,128)})) %all-reduce.7.cloned.1.call-update) | async-done | bytes 131088 | tf_op jit(solution)/shard_map/psum | solution.py:22
  189.1 1.9 convolution_add_fusion.1
  191.2 1.4 fusion.101
  192.6 9.8 %fusion.36 = f32[128,48,128]{0,2,1:T(8,128)} fusion(f32[48,128,128]{2,1,0:T(8,128)S(1)} %copy-done.2, f32[48,128,128]{2,1,0:T(8,128)} %param.18, f32[48]{0:T(128)S(1)} %get-tuple-element.39, pred[48]{0:T(512)(128)(4,1)S(1)} %get-tuple-element.38), kind=kOutput, calls=%fused_computation.34 | convolution fusion | flops 1209532416 | bytes 9437424 | tf_op jit(solution)/shard_map/tsn,skn->tsk/dot_general | solution.py:76
  202.4 3.6 copy.34
  206.0 3.0 fusion.88
  209.1 0.9 fusion.79
  210.0 1.2 fusion.105
  211.2 2.5 gather_fusion.1
  213.8 10.4 %fusion.31 = f32[128,48,128]{0,2,1:T(8,128)} fusion(f32[48,128,128]{2,1,0:T(8,128)} %gather_fusion.1, f32[48,128,128]{2,1,0:T(8,128)} %param.18, f32[48]{0:T(128)S(1)} %get-tuple-element.39, pred[48]{0:T(512)(128)(4,1)S(1)} %compare_and_fusion), kind=kOutput, calls=%fused_computation.33 | convolution fusion | flops 1209532416 | bytes 9437424 | tf_op jit(solution)/shard_map/tsk,skn->tsn/dot_general | solution.py:65
  224.2 3.8 copy.31
  228.0 75.9 %all-reduce.5.cloned.1.call-done = (f32[128,128]{1,0:T(8,128)}, f32[128,128]{1,0:T(8,128)}) async-done(((f32[128,128]{1,0:T(8,128)}, f32[128,128]{1,0:T(8,128)}), (f32[128,128]{1,0:T(8,128)}, f32[128,128]{1,0:T(8,128)})) %all-reduce.5.cloned.1.call-update) | async-done | bytes 131088 | tf_op jit(solution)/shard_map/psum | solution.py:22
  303.9 1.8 convolution_bitcast_fusion
  305.8 3.2 fusion.83
  309.0 2.9 copy.59
  312.0 2.4 gather_fusion.3
  314.5 11.2 %fusion.41 = f32[128,48,128]{0,2,1:T(8,128)} fusion(f32[48,128,128]{2,1,0:T(8,128)} %gather_fusion.3, f32[48,128,128]{2,1,0:T(8,128)} %param.17, f32[48]{0:T(128)S(1)} %get-tuple-element.39, pred[48]{0:T(512)(128)(4,1)S(1)} %compare_and_fusion), kind=kOutput, calls=%fused_computation.35 | convolution fusion | flops 1209532416 | bytes 9437424 | tf_op jit(solution)/shard_map/tsn,skn->tsk/dot_general | solution.py:92
  325.7 4.1 copy.36
  329.7 3.3 fusion.81
  333.0 3.0 copy.58
  336.1 1.0 fusion.107
  337.2 1.9 fusion.100
  339.1 1.4 fusion.106
  340.6 10.0 %fusion.46 = f32[48,128,128]{2,1,0:T(8,128)} fusion(f32[48,128,128]{2,1,0:T(8,128)} %gather_fusion.2, f32[48,128,128]{2,1,0:T(8,128)} %gather_fusion.1, f32[48]{0:T(128)S(1)} %get-tuple-element.39, pred[48]{0:T(512)(128)(4,1)S(1)} %compare_and_fusion, pred[48]{0:T(512)(128)(4,1)S(1)} %get-tuple-element.38), kind=kOutput, calls=%fused_computation.36 | convolution fusion | flops 1210318848 | bytes 9437472 | tf_op jit(solution)/shard_map/tsk,tsn->skn/dot_general | solution.py:84
  350.9 10.0 %fusion.51 = f32[48,128,128]{2,1,0:T(8,128)} fusion(f32[48,128,128]{2,1,0:T(8,128)} %gather_fusion.3, f32[48,128,128]{2,1,0:T(8,128)} %gather_fusion, f32[48]{0:T(128)S(1)} %get-tuple-element.39, pred[48]{0:T(512)(128)(4,1)S(1)} %compare_and_fusion, pred[48]{0:T(512)(128)(4,1)S(1)} %get-tuple-element.38), kind=kOutput, calls=%fused_computation.37 | convolution fusion | flops 1210318848 | bytes 9437472 | tf_op jit(solution)/shard_map/tsk,tsn->skn/dot_general | solution.py:99
  361.0 1.7 copy.39
  362.6 21.3 %reduce-scatter.9.cloned.1.call-done = f32[128,256]{1,0:T(8,128)} async-done(((f32[128,4096]{1,0:T(8,128)}), f32[128,256]{1,0:T(8,128)}) %reduce-scatter.9.cloned.1.call-update) | async-done | bytes 131088 | tf_op jit(solution)/shard_map/reduce_scatter | solution.py:26
  383.9 1.8 convolution_add_fusion.3
  385.7 62.7 %reduce-scatter.11.cloned.1.call-done = f32[128,256]{1,0:T(8,128)} async-done(((f32[128,4096]{1,0:T(8,128)}), f32[128,256]{1,0:T(8,128)}) %reduce-scatter.11.cloned.1.call-update) | async-done | bytes 131088 | tf_op jit(solution)/shard_map/reduce_scatter | solution.py:26
  448.4 1.8 convolution_add_fusion.2
  450.2 10.3 %reduce-scatter.23.cloned.1.call-done = f32[64,256]{1,0:T(8,128)} async-done(((f32[128,256]{1,0:T(8,128)}), f32[64,256]{1,0:T(8,128)}) %reduce-scatter.23.cloned.1.call-update) | async-done | bytes 65552 | tf_op jit(solution)/shard_map/reduce_scatter | solution.py:110
  460.5 17.5 %reduce-scatter.21.cloned.1.call-done = f32[512,128]{1,0:T(8,128)} async-done(((f32[1024,128]{1,0:T(8,128)}), f32[512,128]{1,0:T(8,128)}) %reduce-scatter.21.cloned.1.call-update) | async-done | bytes 262160 | tf_op jit(solution)/shard_map/reduce_scatter | solution.py:109
  478.0 17.3 %reduce-scatter.19.cloned.1.call-done = f32[64,1024]{1,0:T(8,128)} async-done(((f32[128,1024]{1,0:T(8,128)}), f32[64,1024]{1,0:T(8,128)}) %reduce-scatter.19.cloned.1.call-update) | async-done | bytes 262160 | tf_op jit(solution)/shard_map/reduce_scatter | solution.py:108
  495.3 46.3 %reduce-scatter.15.cloned.1.call-done = f32[48,64,128]{2,1,0:T(8,128)} async-done(((f32[48,128,128]{2,1,0:T(8,128)}), f32[48,64,128]{2,1,0:T(8,128)}) %reduce-scatter.15.cloned.1.call-update) | async-done | bytes 1572880 | tf_op jit(solution)/shard_map/reduce_scatter | solution.py:106
  541.6 46.1 %reduce-scatter.13.cloned.1.call-done = f32[48,64,128]{2,1,0:T(8,128)} async-done(((f32[48,128,128]{2,1,0:T(8,128)}), f32[48,64,128]{2,1,0:T(8,128)}) %reduce-scatter.13.cloned.1.call-update) | async-done | bytes 1572880 | tf_op jit(solution)/shard_map/reduce_scatter | solution.py:105
  (61 shorter events, 3.8 us)
Async XLA Ops:
  7.2 184.0 %copy-start = (f32[1024,128]{1,0:T(8,128)S(1)}, f32[1024,128]{1,0:T(8,128)}, u32[]{:S(2)}) copy-start(f32[1024,128]{1,0:T(8,128)} %param.21) | copy-start | bytes 1572868
  7.2 47.8 %all-gather.3.cloned.1.call-start = ((), (), s32[]{:S(2)}) async-start(), calls=%async_computation.8 | async-start | bytes 2228224 | tf_op jit(solution)/shard_map/all_gather | solution.py:18
  9.0 88.9 %all-gather.5.cloned.1.call-start = ((), (), s32[]{:S(2)}) async-start(), calls=%async_computation.10 | async-start | bytes 2228224 | tf_op jit(solution)/shard_map/all_gather | solution.py:18
  10.7 178.4 %all-reduce.7.cloned.1.call-start = ((), (), s32[]{:S(2)}) async-start(), calls=%async_computation.19 | async-start | bytes 262144 | tf_op jit(solution)/shard_map/psum | solution.py:22
  14.5 289.3 %all-reduce.5.cloned.1.call-start = ((), (), s32[]{:S(2)}) async-start(), calls=%async_computation.18 | async-start | bytes 262144 | tf_op jit(solution)/shard_map/psum | solution.py:22
  69.7 3.6 copy-start.12
  99.8 89.3 %copy-start.3 = (f32[128,1024]{1,0:T(8,128)S(1)}, f32[128,1024]{1,0:T(8,128)}, u32[]{:S(2)}) copy-start(f32[128,1024]{1,0:T(8,128)} %param.20) | copy-start | bytes 1572868
  189.1 3.5 copy-start.2
  206.0 3.0 copy-start.13
  213.7 147.2 %reduce-scatter.17.cloned.1.call-start = ((), (), s32[]{:S(2)}) async-start(), calls=%async_computation.14 | async-start | bytes 196608 | tf_op jit(solution)/shard_map/reduce_scatter | solution.py:107
  224.2 79.7 %copy-start.4 = (f32[128,256]{1,0:T(8,128)S(1)}, f32[128,256]{1,0:T(8,128)}, u32[]{:S(2)}) copy-start(f32[128,256]{1,0:T(8,128)} %param.15) | copy-start | bytes 393220
  224.2 81.6 %copy-start.11 = (s32[48]{0:T(128)S(1)}, s32[48]{0:T(128)}, u32[]{:S(2)}) copy-start(s32[48]{0:T(128)} %param.23) | copy-start | bytes 580
  305.7 78.2 %reduce-scatter.9.cloned.1.call-start = ((), (), s32[]{:S(2)}) async-start(), calls=%async_computation.9 | async-start | bytes 2228224 | tf_op jit(solution)/shard_map/reduce_scatter | solution.py:26
  311.9 136.5 %reduce-scatter.11.cloned.1.call-start = ((), (), s32[]{:S(2)}) async-start(), calls=%async_computation.11 | async-start | bytes 2228224 | tf_op jit(solution)/shard_map/reduce_scatter | solution.py:26
  333.0 3.1 copy-start.5
  333.0 3.1 copy-start.10
  336.0 3.1 copy-start.8
  336.0 124.5 %reduce-scatter.23.cloned.1.call-start = ((), (), s32[]{:S(2)}) async-start(), calls=%async_computation.17 | async-start | bytes 196608 | tf_op jit(solution)/shard_map/reduce_scatter | solution.py:110
  337.1 140.9 %reduce-scatter.21.cloned.1.call-start = ((), (), s32[]{:S(2)}) async-start(), calls=%async_computation.16 | async-start | bytes 786432 | tf_op jit(solution)/shard_map/reduce_scatter | solution.py:109
  339.1 156.3 %reduce-scatter.19.cloned.1.call-start = ((), (), s32[]{:S(2)}) async-start(), calls=%async_computation.15 | async-start | bytes 786432 | tf_op jit(solution)/shard_map/reduce_scatter | solution.py:108
  340.6 201.1 %reduce-scatter.15.cloned.1.call-start = ((), (), s32[]{:S(2)}) async-start(), calls=%async_computation.13 | async-start | bytes 4718592 | tf_op jit(solution)/shard_map/reduce_scatter | solution.py:106
  350.6 237.1 %reduce-scatter.13.cloned.1.call-start = ((), (), s32[]{:S(2)}) async-start(), calls=%async_computation.12 | async-start | bytes 4718592 | tf_op jit(solution)/shard_map/reduce_scatter | solution.py:105
  350.9 236.9 %copy-start.1 = (f32[1024,128]{1,0:T(8,128)S(1)}, f32[1024,128]{1,0:T(8,128)}, u32[]{:S(2)}) copy-start(f32[1024,128]{1,0:T(8,128)} %param.21) | copy-start | bytes 1572868
  360.9 23.0 %copy-start.6 = (f32[128,256]{1,0:T(8,128)S(1)}, f32[128,256]{1,0:T(8,128)}, u32[]{:S(2)}) copy-start(f32[128,256]{1,0:T(8,128)} %param.22) | copy-start | bytes 393220
  360.9 87.5 %copy-start.7 = (f32[256,128]{1,0:T(8,128)S(1)}, f32[256,128]{1,0:T(8,128)}, u32[]{:S(2)}) copy-start(f32[256,128]{1,0:T(8,128)} %param.19) | copy-start | bytes 393220
  360.9 87.5 %copy-start.9 = (f32[128,128]{1,0:T(8,128)S(1)}, f32[128,128]{1,0:T(8,128)}, u32[]{:S(2)}) copy-start(f32[128,128]{1,0:T(8,128)} %get-tuple-element.35) | copy-start | bytes 196612
Sparse Core Ops, SparseCore 0:
  10.7 44.1 all-gather.2
  57.7 40.1 all-gather.4
  102.0 87.0 all-reduce.6
  213.8 89.9 all-reduce.4
  306.5 12.0 reduce-scatter.16
  322.1 61.7 reduce-scatter.8
  387.7 60.6 reduce-scatter.10
  451.2 9.3 reduce-scatter.22
  463.4 14.6 reduce-scatter.20
  480.7 14.6 reduce-scatter.18
  498.2 43.4 reduce-scatter.14
  544.3 43.4 reduce-scatter.12
where the time goes:
time: 603 us; the launch traced here: 595 us
  waiting for transfers between devices  442 us (73%)
  matrix products  94.1 us (16%)
  local copies, waits for them, and re-layouts  39.8 us (7%)
  between operations  15.2 us (3%)
    psum x2, waiting for transfers between devices, rank_total(): return lax.psum(partial_value, 'tensor')  163 us
    reduce_scatter x2, waiting for transfers between devices, block_total(): lax.psum_scatter(partial_value, 'tensor', scatter_dimension=1, tiled=True)  83.9 us
    all_gather x2, waiting for transfers between devices, spread_cols(): return lax.all_gather(field, 'tensor', axis=1, tiled=True)  57.8 us
    reduce_scatter x1, waiting for transfers between devices, shards(): lax.psum_scatter(down_grad, 'dp', scatter_dimension=1, tiled=True)  46.3 us
    reduce_scatter x1, waiting for transfers between devices, shards(): lax.psum_scatter(up_grad, 'dp', scatter_dimension=1, tiled=True)  46.1 us
    reduce_scatter x1, waiting for transfers between devices, shards(): lax.psum_scatter(down_left_grad, 'dp', scatter_dimension=0, tiled=True)  17.5 us
    reduce_scatter x1, waiting for transfers between devices, shards(): lax.psum_scatter(up_right_grad, 'dp', scatter_dimension=0, tiled=True)  17.3 us
  transfers between devices with their start and end apart: 12, of which 11 were waited for; matrix products, arithmetic and copies ran while one was open for 18% of the time, Pallas kernels for 0%

commit v1 on v0

--- a/solution.py
+++ b/solution.py
@@ -4,6 +4,24 @@
 from jax.sharding import PartitionSpec as P
 
 highest = lax.Precision.HIGHEST
+
+
+def gather_around(array, axis, dim):
+    ways, here, step = (lax.axis_size(axis), lax.axis_index(axis), array.shape[dim])
+    shape = [n * ways if d == dim else n for d, n in enumerate(array.shape)]
+    full = lax.dynamic_update_slice_in_dim(
+        jnp.zeros(shape, array.dtype), array, here * step, axis=dim
+    )
+    going_up = going_down = array
+    for far in range(1, ways // 2 + 1):
+        going_up = lax.ppermute(going_up, axis, [(d, (d + 1) % ways) for d in range(ways)])
+        full = lax.dynamic_update_slice_in_dim(full, going_up, (here - far) % ways * step, axis=dim)
+        if 2 * far < ways:
+            going_down = lax.ppermute(going_down, axis, [(d, (d - 1) % ways) for d in range(ways)])
+            full = lax.dynamic_update_slice_in_dim(
+                full, going_down, (here + far) % ways * step, axis=dim
+            )
+    return full
 
 
 def activation(values):
@@ -15,7 +33,7 @@
 
 
 def spread_cols(field):
-    return lax.all_gather(field, "tensor", axis=1, tiled=True)
+    return gather_around(field, "tensor", 1)
 
 
 def rank_total(partial_value):

time: 603 us -> 529 us (0.88)
  waiting for transfers between devices: 442 us -> 305 us
  starting transfers between devices: 0.67 us -> 65 us
    psum x2, waiting for transfers between devices: 163 us -> 68.4 us  [rank_total(): return lax.psum(partial_value, 'tensor')]
    ppermute x0 -> x30, starting transfers between devices: none -> 63.8 us  [the longest x14 63.6 us: gather_around(): lax.ppermute(going_down, axis, [(d, (d - 1) % ways) for d in range(ways)])]
    all_gather x2 -> x0, waiting for transfers between devices: 57.8 us -> none  [spread_cols(): return lax.all_gather(field, 'tensor', axis=1, tiled=True)]
    ppermute x0 -> x30, waiting for transfers between devices: none -> 14.1 us  [the longest x16 14 us: gather_around(): lax.ppermute(going_up, axis, [(d, (d + 1) % ways) for d in range(ways)])]
  transfers between devices with their start and end apart: 12 -> 40, of which waited for: 11 -> 12; matrix products, arithmetic and copies ran while one was open for 18% -> 24% of each run, Pallas kernels for 0% -> 0%
where the time goes in v1:
time: 529 us; the launch traced here: 525 us
  waiting for transfers between devices  305 us (58%)
  matrix products  93.5 us (18%)
  starting transfers between devices  65 us (12%)
  local copies, waits for them, and re-layouts  43.5 us (8%)
  between operations  16 us (3%)
    reduce_scatter x2, waiting for transfers between devices, block_total(): lax.psum_scatter(partial_value, 'tensor', scatter_dimension=1, tiled=True)  84.3 us
    psum x2, waiting for transfers between devices, rank_total(): return lax.psum(partial_value, 'tensor')  68.4 us
    ppermute x14, starting transfers between devices, gather_around(): lax.ppermute(going_down, axis, [(d, (d - 1) % ways) for d in range(ways)])  63.6 us
    reduce_scatter x1, waiting for transfers between devices, shards(): lax.psum_scatter(up_grad, 'dp', scatter_dimension=1, tiled=True)  46.3 us
    reduce_scatter x1, waiting for transfers between devices, shards(): lax.psum_scatter(down_grad, 'dp', scatter_dimension=1, tiled=True)  46.1 us
    reduce_scatter x1, waiting for transfers between devices, shards(): lax.psum_scatter(up_right_grad, 'dp', scatter_dimension=0, tiled=True)  17.5 us
    reduce_scatter x1, waiting for transfers between devices, shards(): lax.psum_scatter(down_left_grad, 'dp', scatter_dimension=0, tiled=True)  17.5 us
    ppermute x16, waiting for transfers between devices, gather_around(): lax.ppermute(going_up, axis, [(d, (d + 1) % ways) for d in range(ways)])  14 us
  transfers between devices with their start and end apart: 40, of which 12 were waited for; matrix products, arithmetic and copies ran while one was open for 24% of the time, Pallas kernels for 0%

profile of v1, /device:TPU:0, one launch (start us, length us, event | category | flops | bytes accessed | tf_op | source)
XLA Modules:
  0.0 524.7 jit_solution(2298526887249098254)
XLA Ops:
  8.3 5.5 %collective-permute-start.16 = (f32[128,256]{0,1:T(8,128)S(1)}, f32[128,256]{0,1:T(8,128)S(1)}, u32[]{:S(2)}, u32[]{:S(2)}) collective-permute-start(f32[128,256]{0,1:T(8,128)S(1)} %copy.34), channel_id=1, source_target_pairs={{0,15},{1,0},{2,1},{3,2},{4,3},{5,4},{6,5},{7,6},{8,7},{9,8},{10,9... | collective-permute-start | bytes 393224 | tf_op jit(solution)/shard_map/ppermute | solution.py:20
  14.8 4.5 collective-permute-start.1
  26.4 4.5 collective-permute-start.18
  30.9 4.4 collective-permute-start.3
  35.5 4.5 collective-permute-start.20
  40.0 4.4 collective-permute-start.5
  44.5 4.5 collective-permute-start.22
  49.0 4.4 collective-permute-start.7
  53.6 4.5 collective-permute-start.24
  58.1 4.4 collective-permute-start.9
  62.6 4.5 collective-permute-start.26
  67.1 4.4 collective-permute-start.11
  71.7 4.5 collective-permute-start.28
  76.2 4.4 collective-permute-start.13
  80.7 2.6 collective-permute-done.27
  83.3 4.5 collective-permute-done.12
  88.1 2.3 collective-permute-done.29
  90.4 4.6 collective-permute-done.14
  97.0 1.9 copy.37
  98.9 3.0 copy.28
  101.9 4.0 gather_fusion
  105.9 2.4 gather_fusion.2
  108.3 11.3 %fusion.36 = f32[128,48,128]{0,2,1:T(8,128)} fusion(f32[48,128,128]{2,1,0:T(8,128)} %gather_fusion.2, f32[48,128,128]{2,1,0:T(8,128)} %param.18, f32[48]{0:T(128)S(1)} %compare_convert_fusion, pred[48]{0:T(512)(128)(4,1)S(1)} %get-tuple-element.39), kind=kOutput, calls=%fused_computation.34 | convolution fusion | flops 1209532416 | bytes 9437424 | tf_op jit(solution)/shard_map/tsn,skn->tsk/dot_general | solution.py:94
  119.6 3.7 copy.38
  123.3 3.2 fusion.88
  126.4 8.5 %fusion.26 = f32[128,48,128]{0,2,1:T(8,128)} fusion(f32[48,128,128]{2,1,0:T(8,128)S(1)} %copy-done.2, f32[48,128,128]{2,1,0:T(8,128)} %param.17, f32[48]{0:T(128)S(1)} %compare_convert_fusion, pred[48]{0:T(512)(128)(4,1)S(1)} %get-tuple-element.39), kind=kOutput, calls=%fused_computation.32 | convolution fusion | flops 1209532416 | bytes 9437424 | tf_op jit(solution)/shard_map/tsk,skn->tsn/dot_general | solution.py:75
  135.0 3.8 copy.30
  138.8 3.1 fusion.90
  147.9 2.5 gather_fusion.3
  150.4 11.2 %fusion.41 = f32[128,48,128]{0,2,1:T(8,128)} fusion(f32[48,128,128]{2,1,0:T(8,128)} %gather_fusion.3, f32[48,128,128]{2,1,0:T(8,128)} %param.17, f32[48]{0:T(128)S(1)} %compare_convert_fusion, pred[48]{0:T(512)(128)(4,1)S(1)} %get-tuple-element.38), kind=kOutput, calls=%fused_computation.35 | convolution fusion | flops 1209532416 | bytes 9437424 | tf_op jit(solution)/shard_map/tsn,skn->tsk/dot_general | solution.py:110
  161.6 3.7 copy.40
  165.3 68.4 %all-reduce.5.cloned.1.call-done = (f32[128,128]{1,0:T(8,128)}, f32[128,128]{1,0:T(8,128)}) async-done(((f32[128,128]{1,0:T(8,128)}, f32[128,128]{1,0:T(8,128)}), (f32[128,128]{1,0:T(8,128)}, f32[128,128]{1,0:T(8,128)})) %all-reduce.5.cloned.1.call-update) | async-done | bytes 131088 | tf_op jit(solution)/shard_map/psum | solution.py:40
  235.6 3.2 fusion.81
  238.8 3.0 copy.62
  242.4 2.5 gather_fusion.1
  244.9 10.4 %fusion.31 = f32[128,48,128]{0,2,1:T(8,128)} fusion(f32[48,128,128]{2,1,0:T(8,128)} %gather_fusion.1, f32[48,128,128]{2,1,0:T(8,128)} %param.18, f32[48]{0:T(128)S(1)} %compare_convert_fusion, pred[48]{0:T(512)(128)(4,1)S(1)} %get-tuple-element.38), kind=kOutput, calls=%fused_computation.33 | convolution fusion | flops 1209532416 | bytes 9437424 | tf_op jit(solution)/shard_map/tsk,skn->tsn/dot_general | solution.py:83
  255.3 3.6 copy.33
  258.9 3.3 fusion.83
  262.2 3.0 copy.63
  270.0 10.0 %fusion.51 = f32[48,128,128]{2,1,0:T(8,128)} fusion(f32[48,128,128]{2,1,0:T(8,128)} %gather_fusion.3, f32[48,128,128]{2,1,0:T(8,128)} %gather_fusion, f32[48]{0:T(128)S(1)} %compare_convert_fusion, pred[48]{0:T(512)(128)(4,1)S(1)} %get-tuple-element.38, pred[48]{0:T(512)(128)(4,1)S(1)} %get-tuple-element.39), kind=kOutput, calls=%fused_computation.37 | convolution fusion | flops 1210318848 | bytes 9437472 | tf_op jit(solution)/shard_map/tsk,tsn->skn/dot_general | solution.py:117
  280.3 10.1 %fusion.46 = f32[48,128,128]{2,1,0:T(8,128)} fusion(f32[48,128,128]{2,1,0:T(8,128)} %gather_fusion.2, f32[48,128,128]{2,1,0:T(8,128)} %gather_fusion.1, f32[48]{0:T(128)S(1)} %compare_convert_fusion, pred[48]{0:T(512)(128)(4,1)S(1)} %get-tuple-element.38, pred[48]{0:T(512)(128)(4,1)S(1)} %get-tuple-element.39), kind=kOutput, calls=%fused_computation.36 | convolution fusion | flops 1210318848 | bytes 9437472 | tf_op jit(solution)/shard_map/tsk,tsn->skn/dot_general | solution.py:102
  292.1 21.9 %reduce-scatter.11.cloned.1.call-done = f32[128,256]{1,0:T(8,128)} async-done(((f32[128,4096]{1,0:T(8,128)}), f32[128,256]{1,0:T(8,128)}) %reduce-scatter.11.cloned.1.call-update) | async-done | bytes 131088 | tf_op jit(solution)/shard_map/reduce_scatter | solution.py:44
  315.8 62.5 %reduce-scatter.9.cloned.1.call-done = f32[128,256]{1,0:T(8,128)} async-done(((f32[128,4096]{1,0:T(8,128)}), f32[128,256]{1,0:T(8,128)}) %reduce-scatter.9.cloned.1.call-update) | async-done | bytes 131088 | tf_op jit(solution)/shard_map/reduce_scatter | solution.py:44
  380.1 10.1 %reduce-scatter.23.cloned.1.call-done = f32[64,256]{1,0:T(8,128)} async-done(((f32[128,256]{1,0:T(8,128)}), f32[64,256]{1,0:T(8,128)}) %reduce-scatter.23.cloned.1.call-update) | async-done | bytes 65552 | tf_op jit(solution)/shard_map/reduce_scatter | solution.py:128
  390.2 17.5 %reduce-scatter.21.cloned.1.call-done = f32[512,128]{1,0:T(8,128)} async-done(((f32[1024,128]{1,0:T(8,128)}), f32[512,128]{1,0:T(8,128)}) %reduce-scatter.21.cloned.1.call-update) | async-done | bytes 262160 | tf_op jit(solution)/shard_map/reduce_scatter | solution.py:127
  407.7 17.5 %reduce-scatter.19.cloned.1.call-done = f32[64,1024]{1,0:T(8,128)} async-done(((f32[128,1024]{1,0:T(8,128)}), f32[64,1024]{1,0:T(8,128)}) %reduce-scatter.19.cloned.1.call-update) | async-done | bytes 262160 | tf_op jit(solution)/shard_map/reduce_scatter | solution.py:126
  425.2 46.3 %reduce-scatter.13.cloned.1.call-done = f32[48,64,128]{2,1,0:T(8,128)} async-done(((f32[48,128,128]{2,1,0:T(8,128)}), f32[48,64,128]{2,1,0:T(8,128)}) %reduce-scatter.13.cloned.1.call-update) | async-done | bytes 1572880 | tf_op jit(solution)/shard_map/reduce_scatter | solution.py:123
  471.5 46.1 %reduce-scatter.15.cloned.1.call-done = f32[48,64,128]{2,1,0:T(8,128)} async-done(((f32[48,128,128]{2,1,0:T(8,128)}), f32[48,64,128]{2,1,0:T(8,128)}) %reduce-scatter.15.cloned.1.call-update) | async-done | bytes 1572880 | tf_op jit(solution)/shard_map/reduce_scatter | solution.py:124
  (152 shorter events, 29.7 us)
Async XLA Ops:
  7.2 136.3 %copy-start = (f32[1024,128]{1,0:T(8,128)S(1)}, f32[1024,128]{1,0:T(8,128)}, u32[]{:S(2)}) copy-start(f32[1024,128]{1,0:T(8,128)} %param.21) | copy-start | bytes 1572868
  7.2 134.7 %all-reduce.7.cloned.1.call-start = ((), (), s32[]{:S(2)}) async-start(), calls=%async_computation.17 | async-start | bytes 262144 | tf_op jit(solution)/shard_map/psum | solution.py:40
  8.3 18.2 %collective-permute-start.16 = (f32[128,256]{0,1:T(8,128)S(1)}, f32[128,256]{0,1:T(8,128)S(1)}, u32[]{:S(2)}, u32[]{:S(2)}) collective-permute-start(f32[128,256]{0,1:T(8,128)S(1)} %copy.34), channel_id=1, source_target_pairs={{0,15},{1,0},{2,1},{3,2},{4,3},{5,4},{6,5},{7,6},{8,7},{9,8},{10,9... | collective-permute-start | bytes 393224 | tf_op jit(solution)/shard_map/ppermute | solution.py:20
  13.8 17.2 %collective-permute-start.15 = (f32[128,256]{0,1:T(8,128)S(1)}, f32[128,256]{0,1:T(8,128)S(1)}, u32[]{:S(2)}, u32[]{:S(2)}) collective-permute-start(f32[128,256]{0,1:T(8,128)S(1)} %copy.34), channel_id=1, source_target_pairs={{0,1},{1,2},{2,3},{3,4},{4,5},{5,6},{6,7},{7,8},{8,9},{9,10},{10,1... | collective-permute-start | bytes 393224 | tf_op jit(solution)/shard_map/ppermute | solution.py:17
  14.8 16.2 %collective-permute-start.1 = (f32[128,256]{0,1:T(8,128)S(1)}, f32[128,256]{0,1:T(8,128)S(1)}, u32[]{:S(2)}, u32[]{:S(2)}) collective-permute-start(f32[128,256]{0,1:T(8,128)S(1)} %copy.25), channel_id=1, source_target_pairs={{0,15},{1,0},{2,1},{3,2},{4,3},{5,4},{6,5},{7,6},{8,7},{9,8},{10,9... | collective-permute-start | bytes 393224 | tf_op jit(solution)/shard_map/ppermute | solution.py:20
  19.3 16.1 %collective-permute-start = (f32[128,256]{0,1:T(8,128)S(1)}, f32[128,256]{0,1:T(8,128)S(1)}, u32[]{:S(2)}, u32[]{:S(2)}) collective-permute-start(f32[128,256]{0,1:T(8,128)S(1)} %copy.25), channel_id=1, source_target_pairs={{0,1},{1,2},{2,3},{3,4},{4,5},{5,6},{6,7},{7,8},{8,9},{9,10},{10,1... | collective-permute-start | bytes 393224 | tf_op jit(solution)/shard_map/ppermute | solution.py:17
  23.0 210.7 %all-reduce.5.cloned.1.call-start = ((), (), s32[]{:S(2)}) async-start(), calls=%async_computation.16 | async-start | bytes 262144 | tf_op jit(solution)/shard_map/psum | solution.py:40
  26.4 9.0 %collective-permute-start.18 = (f32[128,256]{0,1:T(8,128)S(1)}, f32[128,256]{0,1:T(8,128)S(1)}, u32[]{:S(2)}, u32[]{:S(2)}) collective-permute-start(f32[128,256]{0,1:T(8,128)S(1)} %collective-permute-done.16), channel_id=1, source_target_pairs={{0,15},{1,0},{2,1},{3,2},{4,3},{5,4},{6,5},{7,6},{8,7},{9,8},{10,9... | collective-permute-start | bytes 393224 | tf_op jit(solution)/shard_map/ppermute | solution.py:20
  30.9 9.0 %collective-permute-start.17 = (f32[128,256]{0,1:T(8,128)S(1)}, f32[128,256]{0,1:T(8,128)S(1)}, u32[]{:S(2)}, u32[]{:S(2)}) collective-permute-start(f32[128,256]{0,1:T(8,128)S(1)} %collective-permute-done.15), channel_id=1, source_target_pairs={{0,1},{1,2},{2,3},{3,4},{4,5},{5,6},{6,7},{7,8},{8,9},{9,10},{10,1... | collective-permute-start | bytes 393224 | tf_op jit(solution)/shard_map/ppermute | solution.py:17
  30.9 9.0 %collective-permute-start.3 = (f32[128,256]{0,1:T(8,128)S(1)}, f32[128,256]{0,1:T(8,128)S(1)}, u32[]{:S(2)}, u32[]{:S(2)}) collective-permute-start(f32[128,256]{0,1:T(8,128)S(1)} %collective-permute-done.1), channel_id=1, source_target_pairs={{0,15},{1,0},{2,1},{3,2},{4,3},{5,4},{6,5},{7,6},{8,7},{9,8},{10,9... | collective-permute-start | bytes 393224 | tf_op jit(solution)/shard_map/ppermute | solution.py:20
  35.4 9.0 %collective-permute-start.2 = (f32[128,256]{0,1:T(8,128)S(1)}, f32[128,256]{0,1:T(8,128)S(1)}, u32[]{:S(2)}, u32[]{:S(2)}) collective-permute-start(f32[128,256]{0,1:T(8,128)S(1)} %collective-permute-done), channel_id=1, source_target_pairs={{0,1},{1,2},{2,3},{3,4},{4,5},{5,6},{6,7},{7,8},{8,9},{9,10},{10,1... | collective-permute-start | bytes 393224 | tf_op jit(solution)/shard_map/ppermute | solution.py:17
  35.5 9.0 %collective-permute-start.20 = (f32[128,256]{0,1:T(8,128)S(1)}, f32[128,256]{0,1:T(8,128)S(1)}, u32[]{:S(2)}, u32[]{:S(2)}) collective-permute-start(f32[128,256]{0,1:T(8,128)S(1)} %collective-permute-done.18), channel_id=1, source_target_pairs={{0,15},{1,0},{2,1},{3,2},{4,3},{5,4},{6,5},{7,6},{8,7},{9,8},{10,9... | collective-permute-start | bytes 393224 | tf_op jit(solution)/shard_map/ppermute | solution.py:20
  40.0 9.0 %collective-permute-start.19 = (f32[128,256]{0,1:T(8,128)S(1)}, f32[128,256]{0,1:T(8,128)S(1)}, u32[]{:S(2)}, u32[]{:S(2)}) collective-permute-start(f32[128,256]{0,1:T(8,128)S(1)} %collective-permute-done.17), channel_id=1, source_target_pairs={{0,1},{1,2},{2,3},{3,4},{4,5},{5,6},{6,7},{7,8},{8,9},{9,10},{10,1... | collective-permute-start | bytes 393224 | tf_op jit(solution)/shard_map/ppermute | solution.py:17
  40.0 9.0 %collective-permute-start.5 = (f32[128,256]{0,1:T(8,128)S(1)}, f32[128,256]{0,1:T(8,128)S(1)}, u32[]{:S(2)}, u32[]{:S(2)}) collective-permute-start(f32[128,256]{0,1:T(8,128)S(1)} %collective-permute-done.3), channel_id=1, source_target_pairs={{0,15},{1,0},{2,1},{3,2},{4,3},{5,4},{6,5},{7,6},{8,7},{9,8},{10,9... | collective-permute-start | bytes 393224 | tf_op jit(solution)/shard_map/ppermute | solution.py:20
  44.4 9.0 %collective-permute-start.4 = (f32[128,256]{0,1:T(8,128)S(1)}, f32[128,256]{0,1:T(8,128)S(1)}, u32[]{:S(2)}, u32[]{:S(2)}) collective-permute-start(f32[128,256]{0,1:T(8,128)S(1)} %collective-permute-done.2), channel_id=1, source_target_pairs={{0,1},{1,2},{2,3},{3,4},{4,5},{5,6},{6,7},{7,8},{8,9},{9,10},{10,1... | collective-permute-start | bytes 393224 | tf_op jit(solution)/shard_map/ppermute | solution.py:17
  44.5 9.0 %collective-permute-start.22 = (f32[128,256]{0,1:T(8,128)S(1)}, f32[128,256]{0,1:T(8,128)S(1)}, u32[]{:S(2)}, u32[]{:S(2)}) collective-permute-start(f32[128,256]{0,1:T(8,128)S(1)} %collective-permute-done.20), channel_id=1, source_target_pairs={{0,15},{1,0},{2,1},{3,2},{4,3},{5,4},{6,5},{7,6},{8,7},{9,8},{10,9... | collective-permute-start | bytes 393224 | tf_op jit(solution)/shard_map/ppermute | solution.py:20
  49.0 9.0 %collective-permute-start.21 = (f32[128,256]{0,1:T(8,128)S(1)}, f32[128,256]{0,1:T(8,128)S(1)}, u32[]{:S(2)}, u32[]{:S(2)}) collective-permute-start(f32[128,256]{0,1:T(8,128)S(1)} %collective-permute-done.19), channel_id=1, source_target_pairs={{0,1},{1,2},{2,3},{3,4},{4,5},{5,6},{6,7},{7,8},{8,9},{9,10},{10,1... | collective-permute-start | bytes 393224 | tf_op jit(solution)/shard_map/ppermute | solution.py:17
  49.0 9.0 %collective-permute-start.7 = (f32[128,256]{0,1:T(8,128)S(1)}, f32[128,256]{0,1:T(8,128)S(1)}, u32[]{:S(2)}, u32[]{:S(2)}) collective-permute-start(f32[128,256]{0,1:T(8,128)S(1)} %collective-permute-done.5), channel_id=1, source_target_pairs={{0,15},{1,0},{2,1},{3,2},{4,3},{5,4},{6,5},{7,6},{8,7},{9,8},{10,9... | collective-permute-start | bytes 393224 | tf_op jit(solution)/shard_map/ppermute | solution.py:20
  53.5 9.0 %collective-permute-start.6 = (f32[128,256]{0,1:T(8,128)S(1)}, f32[128,256]{0,1:T(8,128)S(1)}, u32[]{:S(2)}, u32[]{:S(2)}) collective-permute-start(f32[128,256]{0,1:T(8,128)S(1)} %collective-permute-done.4), channel_id=1, source_target_pairs={{0,1},{1,2},{2,3},{3,4},{4,5},{5,6},{6,7},{7,8},{8,9},{9,10},{10,1... | collective-permute-start | bytes 393224 | tf_op jit(solution)/shard_map/ppermute | solution.py:17
  53.6 9.0 %collective-permute-start.24 = (f32[128,256]{0,1:T(8,128)S(1)}, f32[128,256]{0,1:T(8,128)S(1)}, u32[]{:S(2)}, u32[]{:S(2)}) collective-permute-start(f32[128,256]{0,1:T(8,128)S(1)} %collective-permute-done.22), channel_id=1, source_target_pairs={{0,15},{1,0},{2,1},{3,2},{4,3},{5,4},{6,5},{7,6},{8,7},{9,8},{10,9... | collective-permute-start | bytes 393224 | tf_op jit(solution)/shard_map/ppermute | solution.py:20
  58.1 9.0 %collective-permute-start.23 = (f32[128,256]{0,1:T(8,128)S(1)}, f32[128,256]{0,1:T(8,128)S(1)}, u32[]{:S(2)}, u32[]{:S(2)}) collective-permute-start(f32[128,256]{0,1:T(8,128)S(1)} %collective-permute-done.21), channel_id=1, source_target_pairs={{0,1},{1,2},{2,3},{3,4},{4,5},{5,6},{6,7},{7,8},{8,9},{9,10},{10,1... | collective-permute-start | bytes 393224 | tf_op jit(solution)/shard_map/ppermute | solution.py:17
  58.1 9.0 %collective-permute-start.9 = (f32[128,256]{0,1:T(8,128)S(1)}, f32[128,256]{0,1:T(8,128)S(1)}, u32[]{:S(2)}, u32[]{:S(2)}) collective-permute-start(f32[128,256]{0,1:T(8,128)S(1)} %collective-permute-done.7), channel_id=1, source_target_pairs={{0,15},{1,0},{2,1},{3,2},{4,3},{5,4},{6,5},{7,6},{8,7},{9,8},{10,9... | collective-permute-start | bytes 393224 | tf_op jit(solution)/shard_map/ppermute | solution.py:20
  62.5 9.0 %collective-permute-start.8 = (f32[128,256]{0,1:T(8,128)S(1)}, f32[128,256]{0,1:T(8,128)S(1)}, u32[]{:S(2)}, u32[]{:S(2)}) collective-permute-start(f32[128,256]{0,1:T(8,128)S(1)} %collective-permute-done.6), channel_id=1, source_target_pairs={{0,1},{1,2},{2,3},{3,4},{4,5},{5,6},{6,7},{7,8},{8,9},{9,10},{10,1... | collective-permute-start | bytes 393224 | tf_op jit(solution)/shard_map/ppermute | solution.py:17
  62.6 9.0 %collective-permute-start.26 = (f32[128,256]{0,1:T(8,128)S(1)}, f32[128,256]{0,1:T(8,128)S(1)}, u32[]{:S(2)}, u32[]{:S(2)}) collective-permute-start(f32[128,256]{0,1:T(8,128)S(1)} %collective-permute-done.24), channel_id=1, source_target_pairs={{0,15},{1,0},{2,1},{3,2},{4,3},{5,4},{6,5},{7,6},{8,7},{9,8},{10,9... | collective-permute-start | bytes 393224 | tf_op jit(solution)/shard_map/ppermute | solution.py:20
  67.1 9.0 %collective-permute-start.25 = (f32[128,256]{0,1:T(8,128)S(1)}, f32[128,256]{0,1:T(8,128)S(1)}, u32[]{:S(2)}, u32[]{:S(2)}) collective-permute-start(f32[128,256]{0,1:T(8,128)S(1)} %collective-permute-done.23), channel_id=1, source_target_pairs={{0,1},{1,2},{2,3},{3,4},{4,5},{5,6},{6,7},{7,8},{8,9},{9,10},{10,1... | collective-permute-start | bytes 393224 | tf_op jit(solution)/shard_map/ppermute | solution.py:17
  67.1 9.0 %collective-permute-start.11 = (f32[128,256]{0,1:T(8,128)S(1)}, f32[128,256]{0,1:T(8,128)S(1)}, u32[]{:S(2)}, u32[]{:S(2)}) collective-permute-start(f32[128,256]{0,1:T(8,128)S(1)} %collective-permute-done.9), channel_id=1, source_target_pairs={{0,15},{1,0},{2,1},{3,2},{4,3},{5,4},{6,5},{7,6},{8,7},{9,8},{10,9... | collective-permute-start | bytes 393224 | tf_op jit(solution)/shard_map/ppermute | solution.py:20
  71.6 9.0 %collective-permute-start.10 = (f32[128,256]{0,1:T(8,128)S(1)}, f32[128,256]{0,1:T(8,128)S(1)}, u32[]{:S(2)}, u32[]{:S(2)}) collective-permute-start(f32[128,256]{0,1:T(8,128)S(1)} %collective-permute-done.8), channel_id=1, source_target_pairs={{0,1},{1,2},{2,3},{3,4},{4,5},{5,6},{6,7},{7,8},{8,9},{9,10},{10,1... | collective-permute-start | bytes 393224 | tf_op jit(solution)/shard_map/ppermute | solution.py:17
  71.7 16.3 %collective-permute-start.28 = (f32[128,256]{0,1:T(8,128)S(1)}, f32[128,256]{0,1:T(8,128)S(1)}, u32[]{:S(2)}, u32[]{:S(2)}) collective-permute-start(f32[128,256]{0,1:T(8,128)S(1)} %collective-permute-done.26), channel_id=1, source_target_pairs={{0,15},{1,0},{2,1},{3,2},{4,3},{5,4},{6,5},{7,6},{8,7},{9,8},{10,9... | collective-permute-start | bytes 393224 | tf_op jit(solution)/shard_map/ppermute | solution.py:20
  76.2 7.1 %collective-permute-start.27 = (f32[128,256]{0,1:T(8,128)S(1)}, f32[128,256]{0,1:T(8,128)S(1)}, u32[]{:S(2)}, u32[]{:S(2)}) collective-permute-start(f32[128,256]{0,1:T(8,128)S(1)} %collective-permute-done.25), channel_id=1, source_target_pairs={{0,1},{1,2},{2,3},{3,4},{4,5},{5,6},{6,7},{7,8},{8,9},{9,10},{10,1... | collective-permute-start | bytes 393224 | tf_op jit(solution)/shard_map/ppermute | solution.py:17
  76.2 11.8 %collective-permute-start.13 = (f32[128,256]{0,1:T(8,128)S(1)}, f32[128,256]{0,1:T(8,128)S(1)}, u32[]{:S(2)}, u32[]{:S(2)}) collective-permute-start(f32[128,256]{0,1:T(8,128)S(1)} %collective-permute-done.11), channel_id=1, source_target_pairs={{0,15},{1,0},{2,1},{3,2},{4,3},{5,4},{6,5},{7,6},{8,7},{9,8},{10,9... | collective-permute-start | bytes 393224 | tf_op jit(solution)/shard_map/ppermute | solution.py:20
  80.6 7.1 %collective-permute-start.12 = (f32[128,256]{0,1:T(8,128)S(1)}, f32[128,256]{0,1:T(8,128)S(1)}, u32[]{:S(2)}, u32[]{:S(2)}) collective-permute-start(f32[128,256]{0,1:T(8,128)S(1)} %collective-permute-done.10), channel_id=1, source_target_pairs={{0,1},{1,2},{2,3},{3,4},{4,5},{5,6},{6,7},{7,8},{8,9},{9,10},{10,1... | collective-permute-start | bytes 393224 | tf_op jit(solution)/shard_map/ppermute | solution.py:17
  83.3 7.1 %collective-permute-start.29 = (f32[128,256]{0,1:T(8,128)S(1)}, f32[128,256]{0,1:T(8,128)S(1)}, u32[]{:S(2)}, u32[]{:S(2)}) collective-permute-start(f32[128,256]{0,1:T(8,128)S(1)} %collective-permute-done.27), channel_id=1, source_target_pairs={{0,1},{1,2},{2,3},{3,4},{4,5},{5,6},{6,7},{7,8},{8,9},{9,10},{10,1... | collective-permute-start | bytes 393224 | tf_op jit(solution)/shard_map/ppermute | solution.py:17
  87.8 7.2 %collective-permute-start.14 = (f32[128,256]{0,1:T(8,128)S(1)}, f32[128,256]{0,1:T(8,128)S(1)}, u32[]{:S(2)}, u32[]{:S(2)}) collective-permute-start(f32[128,256]{0,1:T(8,128)S(1)} %collective-permute-done.12), channel_id=1, source_target_pairs={{0,1},{1,2},{2,3},{3,4},{4,5},{5,6},{6,7},{7,8},{8,9},{9,10},{10,1... | collective-permute-start | bytes 393224 | tf_op jit(solution)/shard_map/ppermute | solution.py:17
  147.9 142.5 %reduce-scatter.17.cloned.1.call-start = ((), (), s32[]{:S(2)}) async-start(), calls=%async_computation.12 | async-start | bytes 196608 | tf_op jit(solution)/shard_map/reduce_scatter | solution.py:125
  161.6 72.1 %copy-start.6 = (f32[128,256]{1,0:T(8,128)S(1)}, f32[128,256]{1,0:T(8,128)}, u32[]{:S(2)}) copy-start(f32[128,256]{1,0:T(8,128)} %param.15) | copy-start | bytes 393220
  161.6 74.0 %copy-start.14 = (s32[48]{0:T(128)S(1)}, s32[48]{0:T(128)}, u32[]{:S(2)}) copy-start(s32[48]{0:T(128)} %param.23) | copy-start | bytes 580
  235.5 78.4 %reduce-scatter.11.cloned.1.call-start = ((), (), s32[]{:S(2)}) async-start(), calls=%async_computation.9 | async-start | bytes 2228224 | tf_op jit(solution)/shard_map/reduce_scatter | solution.py:44
  241.8 136.4 %reduce-scatter.9.cloned.1.call-start = ((), (), s32[]{:S(2)}) async-start(), calls=%async_computation.8 | async-start | bytes 2228224 | tf_op jit(solution)/shard_map/reduce_scatter | solution.py:44
  262.2 4.1 copy-start.15
  265.2 125.0 %reduce-scatter.23.cloned.1.call-start = ((), (), s32[]{:S(2)}) async-start(), calls=%async_computation.15 | async-start | bytes 196608 | tf_op jit(solution)/shard_map/reduce_scatter | solution.py:128
  266.3 141.4 %reduce-scatter.21.cloned.1.call-start = ((), (), s32[]{:S(2)}) async-start(), calls=%async_computation.14 | async-start | bytes 786432 | tf_op jit(solution)/shard_map/reduce_scatter | solution.py:127
  268.3 156.9 %reduce-scatter.19.cloned.1.call-start = ((), (), s32[]{:S(2)}) async-start(), calls=%async_computation.13 | async-start | bytes 786432 | tf_op jit(solution)/shard_map/reduce_scatter | solution.py:126
  269.8 201.7 %reduce-scatter.13.cloned.1.call-start = ((), (), s32[]{:S(2)}) async-start(), calls=%async_computation.10 | async-start | bytes 4718592 | tf_op jit(solution)/shard_map/reduce_scatter | solution.py:123
  280.0 237.6 %reduce-scatter.15.cloned.1.call-start = ((), (), s32[]{:S(2)}) async-start(), calls=%async_computation.11 | async-start | bytes 4718592 | tf_op jit(solution)/shard_map/reduce_scatter | solution.py:124
  280.3 237.3 %copy-start.1 = (f32[1024,128]{1,0:T(8,128)S(1)}, f32[1024,128]{1,0:T(8,128)}, u32[]{:S(2)}) copy-start(f32[1024,128]{1,0:T(8,128)} %param.21) | copy-start | bytes 1572868
  290.3 23.6 %copy-start.8 = (f32[256,128]{1,0:T(8,128)S(1)}, f32[256,128]{1,0:T(8,128)}, u32[]{:S(2)}) copy-start(f32[256,128]{1,0:T(8,128)} %param.19) | copy-start | bytes 393220
  290.4 23.6 %copy-start.12 = (f32[128,128]{1,0:T(8,128)S(1)}, f32[128,128]{1,0:T(8,128)}, u32[]{:S(2)}) copy-start(f32[128,128]{1,0:T(8,128)} %get-tuple-element.35) | copy-start | bytes 196612
  290.4 87.9 %copy-start.9 = (f32[128,256]{1,0:T(8,128)S(1)}, f32[128,256]{1,0:T(8,128)}, u32[]{:S(2)}) copy-start(f32[128,256]{1,0:T(8,128)} %param.22) | copy-start | bytes 393220
  (8 other events, 22.5 us)
Sparse Core Ops, SparseCore 0:
  23.2 90.9 all-reduce.6
  148.0 85.6 all-reduce.4
  236.5 12.0 reduce-scatter.16
  252.1 61.7 reduce-scatter.10
  317.5 60.6 reduce-scatter.8
  380.9 9.2 reduce-scatter.22
  393.0 14.6 reduce-scatter.20
  410.5 14.6 reduce-scatter.18
  428.0 43.4 reduce-scatter.12
  474.2 43.4 reduce-scatter.14
